TPU v7x, 32 devices: a whole 2x2x4 slice. The times are simulated.
32 devices in a mesh: grp: 4 (over y, x), dev: 8 (over z, core).
Axes of the slice: x: 2, y: 2, z: 4, core: 2. Of those that a mesh axis runs over, the one named last changes fastest.
Arguments:
- raw: bfloat16 [128, 16, 4096], P(('grp', 'dev'))
- dark: bfloat16 [16, 4096], replicated, may hold values from 0.049804688 to 0.29882812
- basis: bfloat16 [8, 4096], replicated, may hold values from -3 to 3
- counts: int32 [128], P(('grp', 'dev')), may hold values from 1 to 16, as said below
- positions: int32 [128], replicated, may hold values from 0 to 127, as said below
Outputs:
- corrected: bfloat16 [128, 16, 4096], P(('grp', 'dev'))
- pooled: bfloat16 [4, 16, 1, 30720], P('grp', None, None, 'dev')
Inputs may be any that keep to these rules, and one draw needn't show every extreme that they name: `counts`: the first tile of every device (4 tiles in acquisition order) has all 16 planes. A permutation of the tile positions of the slide image. The 4 tiles of the device at grp index g and dev index d lie in 4 different bands, all at tile columns d * 4 to d * 4 + 3.
All inputs are finite; a program needn't handle non-finite values.
Results may differ from a plain program's by a relative error of at most 0.0046.
Values may be sent and summed in bfloat16 or wider, within the bound.
A program may use at most 128 MiB of HBM per device.

v0:
```python
import jax
import jax.numpy as jnp
from jax import lax
from jax.sharding import PartitionSpec as P

ROWS = 2
COLS = 2048
OVL = 128


def shifted(value, axis, steps):
    count = lax.axis_size(axis)
    first, last = (max(0, -steps), min(count, count - steps))
    return lax.ppermute(value, axis, [(source, source + steps) for source in range(first, last)])


def feather():
    column = jnp.arange(COLS, dtype=jnp.float32) + 0.5
    return jnp.minimum(1.0, jnp.minimum(column / OVL, (COLS - column) / OVL))


def pooling(tiles):
    count = tiles.shape[0]
    planes = tiles.shape[1]
    shaped = tiles.reshape(count, planes, ROWS, COLS) * feather()
    return jnp.sum(shaped.reshape(count, planes, ROWS // 2, 2, COLS // 2, 2), axis=(3, 5)) * 0.25


def per_device(raw, dark, basis, counts, positions):
    tile_count, planes, pixels = raw.shape
    groups = lax.axis_size("grp")
    columns = lax.axis_size("dev")
    band_size = columns * tile_count
    live = (jnp.arange(planes, dtype=jnp.int32)[None, :] < counts[:, None]).astype(jnp.float32)
    projected = jnp.einsum("kx,tpx->tkp", basis, raw, preferred_element_type=jnp.float32)
    local_proj = jnp.sum(projected * live[:, None, :], axis=0)
    ones_row = jnp.ones((pixels,), jnp.bfloat16)
    local_sum = jnp.sum(
        jnp.einsum("tpx,x->tp", raw, ones_row, preferred_element_type=jnp.float32) * live, axis=0
    )
    local_live = jnp.sum(live, axis=0)
    proj, total, alive = lax.psum((local_proj, local_sum, local_live), ("grp", "dev"))
    dark_f = dark.astype(jnp.float32)
    dark_proj = jnp.dot(basis, dark.T, preferred_element_type=jnp.float32)
    dark_sum = jnp.sum(dark_f, axis=1)
    coef = (proj - alive[None, :] * dark_proj) / (total - alive * dark_sum)[None, :]
    shade = jnp.dot(coef.T, basis.astype(jnp.float32), precision=lax.Precision.HIGHEST)
    inverse = jnp.exp(-shade)
    corrected = (
        (raw.astype(jnp.float32) - dark_f[None]) * inverse[None] * live[:, :, None]
    ).astype(jnp.bfloat16)
    here_grp = lax.axis_index("grp")
    here_dev = lax.axis_index("dev")
    layout = positions.reshape(groups, columns, tile_count)
    mine = lax.dynamic_index_in_dim(
        lax.dynamic_index_in_dim(layout, here_grp, 0, False), here_dev, 0, False
    )
    select = mine[None, :] // band_size == jnp.arange(groups, dtype=jnp.int32)[:, None]
    column_tiles = lax.dynamic_index_in_dim(layout, here_dev, 1, False)
    arrives = column_tiles // band_size == here_grp
    slot_of = jnp.sum(jnp.where(arrives, column_tiles % tile_count, 0), axis=1)
    place = slot_of[None, :] == jnp.arange(tile_count, dtype=jnp.int32)[:, None]
    own_cells = (
        pooling(corrected.astype(jnp.float32))
        .astype(jnp.bfloat16)
        .reshape(tile_count, planes, ROWS // 2 * (COLS // 2))
    )
    outgoing = jnp.einsum(
        "bs,spx->bpx", select.astype(jnp.bfloat16), own_cells, preferred_element_type=jnp.float32
    ).astype(jnp.bfloat16)
    arrived = lax.all_to_all(outgoing, "grp", split_axis=0, concat_axis=0, tiled=True)
    placed = jnp.einsum(
        "jb,bpx->jpx", place.astype(jnp.bfloat16), arrived, preferred_element_type=jnp.float32
    ).astype(jnp.bfloat16)
    cells = placed.reshape(tile_count, planes, ROWS // 2, COLS // 2)
    cells = lax.optimization_barrier(cells)
    half_step = (COLS - OVL) // 2
    half_ovl = OVL // 2
    head = cells[..., :half_step].astype(jnp.float32)
    tail = cells[..., half_step:]
    spill = shifted(tail[-1], "dev", 1)
    carried = jnp.concatenate([spill[None], tail[:-1]], axis=0)
    carried = jnp.pad(carried, ((0, 0), (0, 0), (0, 0), (0, half_step - half_ovl))).astype(
        jnp.float32
    )
    merged = head + carried
    result = jnp.transpose(merged, (1, 2, 0, 3)).reshape(
        1, planes, ROWS // 2, tile_count * half_step
    )
    return (corrected, result.astype(jnp.bfloat16))


def solution(mesh):
    in_specs = (P(("grp", "dev"), None, None), P(), P(), P(("grp", "dev")), P())
    out_specs = (P(("grp", "dev"), None, None), P("grp", None, None, "dev"))
    return jax.shard_map(
        per_device, mesh=mesh, in_specs=in_specs, out_specs=out_specs, check_vma=False
    )
```

profile of v0, /device:TPU:1, one launch (start us, length us, event | category | flops | bytes accessed | tf_op | source)
XLA Modules:
  0.0 94.8 jit_solution(9570556487243521192)
XLA Ops:
  0.6 0.0 copy-start
  0.6 1.1 %convert_reduce_fusion = f32[16]{0:T(128)S(1)} fusion(bf16[16,4096]{1,0:T(8,128)(2,1)} %param.6), kind=kLoop, calls=%fused_computation.22 | loop fusion | flops 131056 | bytes 131136 | tf_op jit(solution)/shard_map/reduce_sum | solution.py:45
  1.7 0.9 convert_element_type.62
  2.7 0.7 fusion.18
  3.4 1.7 %fusion.12 = f32[1,4,16]{2,0,1:T(1,128)S(1)} fusion(bf16[4,16,4096]{2,1,0:T(8,128)(2,1)} %param.5), kind=kOutput, calls=%fused_computation.23 | convolution fusion | flops 524288 | bytes 524544 | tf_op jit(solution)/shard_map/tpx,x->tp/dot_general | solution.py:39
  5.2 0.8 fusion.26
  5.9 0.0 copy-done
  5.9 1.8 %fusion.2 = f32[16,8]{0,1:T(8,128)S(1)} fusion(bf16[4,16,4096]{2,1,0:T(8,128)(2,1)} %param.5, bf16[8,4096]{1,0:T(8,128)(2,1)S(1)} %copy-done, f32[4,16]{1,0:T(4,128)S(1)} %fusion.18), kind=kOutput, calls=%fused_computation.7 | convolution fusion | flops 4195200 | bytes 590592 | tf_op jit(solution)/shard_map/kx,tpx->tkp/dot_general | solution.py:35
  7.7 40.5 %all-reduce.1 = (f32[8,16]{1,0:T(8,128)S(1)}, f32[16]{0:T(128)S(1)}, f32[16]{0:T(128)S(1)}) all-reduce(f32[8,16]{1,0:T(8,128)S(1)} %bitcast.39, f32[16]{0:T(128)S(1)} %get-tuple-element.3, f32[16]{0:T(128)S(1)} %get-tuple-element.2), channel_id=1, replica_groups=mesh['grp'=4,'dev'=8] {'grp','dev'}, use_global_device_ids=true, to_apply=%region_1.0 | all-reduce | flops 160 | bytes 1280 | tf_op jit(solution)/shard_map/psum | solution.py:42
  48.2 1.1 %fusion.4 = f32[8,16]{1,0:T(8,128)S(1)} fusion(f32[8,16]{1,0:T(8,128)S(1)} %get-tuple-element.4, bf16[8,4096]{1,0:T(8,128)(2,1)S(1)} %copy-done, bf16[16,4096]{1,0:T(8,128)(2,1)} %param.6, f32[16]{0:T(128)S(1)} %multiply_subtract_fusion, f32[16]{0:T(128)S(1)} %get-tuple-element.6), kind=kOutput, calls=%fused_computation.10 | convolution fusion | flops 1048960 | bytes 197760 | tf_op jit(solution)/shard_map/dot_general | solution.py:44
  49.3 0.3 fusion
  49.6 1.2 %multiply_convert_fusion = bf16[4,16,4096]{2,1,0:T(8,128)(2,1)S(1)} fusion(bf16[4,16,4096]{2,1,0:T(8,128)(2,1)} %param.5, f32[4,16]{1,0:T(4,128)S(1)} %fusion.18, f32[16,4096]{1,0:T(8,128)S(1)} %fusion, f32[16,4096]{1,0:T(8,128)S(1)} %convert_element_type.62), kind=kLoop, calls=%fused_computation.11 | loop fusion | flops 1310720 | bytes 1573120 | tf_op jit(solution)/shard_map/convert_element_type | solution.py:51
  50.9 0.0 copy-start.1
  50.9 4.1 %copy.17 = f32[4,16,4096]{1,2,0:T(8,128)} copy(bf16[4,16,4096]{2,1,0:T(8,128)(2,1)S(1)} %multiply_convert_fusion) | data formatting | bytes 1572864 | tf_op jit(solution)/shard_map/reshape | solution.py:25
  54.9 0.0 copy-start.2
  54.9 0.2 copy.18
  55.2 23.0 %multiply_reduce_fusion = f32[4,16,1024]{1,2,0:T(8,128)S(1)} fusion(f32[4,16,1,2,1024,2]{1,5,4,3,0,2:T(2,128)} %bitcast.38, f32[1024,2]{1,0:T(8,128)S(1)} %copy.18), kind=kLoop, calls=%fused_computation | loop fusion | flops 458752 | bytes 1318912 | tf_op jit(solution)/shard_map/reduce_sum | solution.py:26
  78.1 0.0 copy-done.1
  78.1 0.6 copy.19
  78.7 0.0 copy-done.2
  78.8 0.1 reshape.162
  78.9 0.2 convolution_convert_fusion.1
  79.1 0.7 copy.21
  79.8 3.3 %all-to-all-start = ((bf16[4,16,1024]{2,1,0:T(8,128)(2,1)}), bf16[4,16,1024]{2,1,0:T(8,128)(2,1)S(1)}, u32[]{:S(2)}, u32[]{:S(2)}) async-start(bf16[4,16,1024]{2,1,0:T(8,128)(2,1)} %copy.21), calls=%async_computation | async-start | bytes 262144 | tf_op jit(solution)/shard_map/all_to_all | solution.py:71
  83.1 0.1 fusion.17
  83.3 3.7 %all-to-all-done = bf16[4,16,1024]{2,1,0:T(8,128)(2,1)S(1)} async-done(((bf16[4,16,1024]{2,1,0:T(8,128)(2,1)}), bf16[4,16,1024]{2,1,0:T(8,128)(2,1)S(1)}, u32[]{:S(2)}, u32[]{:S(2)}) %all-to-all-start) | async-done | bytes 131104 | tf_op jit(solution)/shard_map/all_to_all | solution.py:71
  87.0 0.2 fusion.1
  87.2 0.1 slice.16
  87.3 5.9 %collective-permute-start = (bf16[16,1,64]{2,0,1:T(8,128)(2,1)S(1)}, bf16[16,1,64]{2,0,1:T(8,128)(2,1)S(1)}, u32[]{:S(2)}, u32[]{:S(2)}) collective-permute-start(bf16[16,1,64]{2,0,1:T(8,128)(2,1)S(1)} %bitcast.42), channel_id=1, source_target_pairs={{0,1},{1,2},{2,3},{3,4},{4,5},{5,6},{6,7},{8,9},{9,10},{10,11},{11... | collective-permute-start | bytes 6152 | tf_op jit(solution)/shard_map/ppermute | solution.py:14
  93.2 0.1 slice.17
  93.3 0.6 collective-permute-done
  93.9 0.1 fusion.7
  94.0 0.8 convert_element_type.72
  (7 shorter events, 0.1 us)
Async XLA Ops:
  0.6 5.3 %copy-start = (bf16[8,4096]{1,0:T(8,128)(2,1)S(1)}, bf16[8,4096]{1,0:T(8,128)(2,1)}, u32[]{:S(2)}) copy-start(bf16[8,4096]{1,0:T(8,128)(2,1)} %param.7) | copy-start | bytes 196612
  50.9 27.3 %copy-start.1 = (bf16[4,16,4096]{2,1,0:T(8,128)(2,1)}, bf16[4,16,4096]{2,1,0:T(8,128)(2,1)S(1)}, u32[]{:S(2)}) copy-start(bf16[4,16,4096]{2,1,0:T(8,128)(2,1)S(1)} %multiply_convert_fusion) | copy-start | bytes 1572868
  54.9 23.8 %copy-start.2 = (s32[128]{0:T(128)S(1)}, s32[128]{0:T(128)}, u32[]{:S(2)}) copy-start(s32[128]{0:T(128)} %param.9) | copy-start | bytes 1540
  79.8 7.2 %all-to-all-start = ((bf16[4,16,1024]{2,1,0:T(8,128)(2,1)}), bf16[4,16,1024]{2,1,0:T(8,128)(2,1)S(1)}, u32[]{:S(2)}, u32[]{:S(2)}) async-start(bf16[4,16,1024]{2,1,0:T(8,128)(2,1)} %copy.21), calls=%async_computation | async-start | bytes 262144 | tf_op jit(solution)/shard_map/all_to_all | solution.py:71
  87.3 6.7 %collective-permute-start = (bf16[16,1,64]{2,0,1:T(8,128)(2,1)S(1)}, bf16[16,1,64]{2,0,1:T(8,128)(2,1)S(1)}, u32[]{:S(2)}, u32[]{:S(2)}) collective-permute-start(bf16[16,1,64]{2,0,1:T(8,128)(2,1)S(1)} %bitcast.42), channel_id=1, source_target_pairs={{0,1},{1,2},{2,3},{3,4},{4,5},{5,6},{6,7},{8,9},{9,10},{10,11},{11... | collective-permute-start | bytes 6152 | tf_op jit(solution)/shard_map/ppermute | solution.py:14
where the time goes:
time: 95.3 us; the launch traced here: 94.8 us
  blocking collectives  40.5 us (42%)
  other arithmetic  27.9 us (29%)
  starting transfers between devices  9.24 us (10%)
  local copies, waits for them, and re-layouts  6.65 us (7%)
  matrix products  5.32 us (6%)
  waiting for transfers between devices  4.34 us (5%)
    psum x1, blocking collectives, per_device(): lax.psum((local_proj, local_sum, local_live), ('grp', 'dev'))  40.5 us
    reduce_sum x1, other arithmetic, pooling(): jnp.sum(shaped.reshape(count, planes, ROWS // 2, 2, COLS // 2, 2), axis=(...  23 us
    ppermute x1, starting transfers between devices, shifted(): lax.ppermute(value, axis, [(source, source + steps) for source in range(f...  5.91 us
    reshape x1, local copies, waits for them, and re-layouts, pooling(): shaped = tiles.reshape(count, planes, ROWS, COLS) * feather()  4.06 us
    all_to_all x1, waiting for transfers between devices, per_device(): lax.all_to_all(outgoing, 'grp', split_axis=0, concat_axis=0, tiled=True)  3.7 us
    all_to_all x1, starting transfers between devices, per_device(): lax.all_to_all(outgoing, 'grp', split_axis=0, concat_axis=0, tiled=True)  3.32 us
  transfers between devices with their start and end apart: 2, of which 2 were waited for; matrix products, arithmetic and copies ran while one was open for 0% of the time, Pallas kernels for 0%

commit v1 on v0

v1 whole, which is shorter than its diff:
```python
import functools

import jax
import jax.numpy as jnp
from jax import lax
from jax.experimental import pallas as pl
from jax.experimental.pallas import tpu as pltpu
from jax.sharding import PartitionSpec as P

ROWS = 2
COLS = 2048
OVL = 128
LANES = 128
BLOCK = 256
MESH = pl.DeviceIdType.MESH
NT = (((1,), (1,)), ((), ()))


def pool_weights(block, blocks):
    row = lax.broadcasted_iota(jnp.int32, (BLOCK, LANES), 0)
    lane = lax.broadcasted_iota(jnp.int32, (BLOCK, LANES), 1)
    column = (row + block * BLOCK).astype(jnp.float32) + 0.5
    ramp = jnp.minimum(1.0, jnp.minimum(column / OVL, (blocks * BLOCK - column) / OVL))
    inside = (row >= 2 * lane) & (row < 2 * lane + 2)
    return jnp.where(inside, 0.25 * ramp, 0.0).astype(jnp.bfloat16)


def kernel(
    groups, columns,
    counts_ref, positions_ref, raw_ref, dark_ref, basis_ref,
    corrected_ref, pooled_ref,
    rhs, stat, grp_buf, dev_buf, weights, outgoing, arrived, tail_out, tail_in, acc,
    grp_send, grp_recv, dev_send, dev_recv, cell_send, cell_recv, tail_send, tail_recv,
):
    tiles, planes, pixels = raw_ref.shape
    rank = basis_ref.shape[0]
    band_size = columns * tiles
    half_step = (COLS - OVL) // 2
    half_ovl = OVL // 2
    cells_wide = COLS // 2
    last = cells_wide - LANES
    blocks = COLS // BLOCK
    g = lax.axis_index("grp")
    d = lax.axis_index("dev")

    barrier = pltpu.get_barrier_semaphore()
    near = [lax.rem(d + 1, columns), lax.rem(d + columns - 1, columns)]
    for o in range(1, groups):
        other = lax.rem(g + o, groups)
        for where in [d] + near:
            pl.semaphore_signal(barrier, inc=1, device_id=(other, where), device_id_type=MESH)
    for o in range(1, columns):
        pl.semaphore_signal(
            barrier, inc=1, device_id=(g, lax.rem(d + o, columns)), device_id_type=MESH
        )

    rhs[0:rank, :] = basis_ref[...]
    rhs[rank:, :] = jnp.ones((rhs.shape[0] - rank, pixels), jnp.bfloat16)
    width = rhs.shape[0]
    sums = lax.dot_general(
        raw_ref[...].reshape(tiles * planes, pixels), rhs[...], NT,
        preferred_element_type=jnp.float32,
    )
    dark_sums = lax.dot_general(dark_ref[...], rhs[...], NT, preferred_element_type=jnp.float32)
    plane = lax.broadcasted_iota(jnp.int32, (planes, width), 0)
    local = jnp.zeros((planes, width), jnp.float32)
    for t in range(tiles):
        part = sums[t * planes:(t + 1) * planes] - dark_sums
        local = local + jnp.where(plane < counts_ref[t], part, 0.0)
    stat[...] = jnp.zeros_like(stat)
    stat[:, 0:width] = local
    half = planes // 2
    grp_buf[g] = stat[0:half, :] + pltpu.roll(stat[half:, :], LANES // 2, 1)

    pl.semaphore_wait(barrier, 3 * (groups - 1) + columns - 1)

    copies = []
    for o in range(1, groups):
        other = lax.rem(g + o, groups)
        copy = pltpu.make_async_remote_copy(
            src_ref=grp_buf.at[g], dst_ref=grp_buf.at[g],
            send_sem=grp_send.at[o], recv_sem=grp_recv.at[g],
            device_id=(other, d), device_id_type=MESH,
        )
        copy.start()
        copies.append(copy)
    weights[0] = pool_weights(0, blocks)
    weights[1] = pool_weights(1, blocks)
    weights[2] = pool_weights(blocks - 1, blocks)
    for o in range(1, groups):
        source = lax.rem(g + groups - o, groups)
        pltpu.make_async_remote_copy(
            src_ref=grp_buf.at[source], dst_ref=grp_buf.at[source],
            send_sem=grp_send.at[o], recv_sem=grp_recv.at[source],
            device_id=(source, d), device_id_type=MESH,
        ).wait_recv()
    for copy in copies:
        copy.wait_send()
    dev_buf[d] = jnp.sum(grp_buf[...], axis=0)
    copies = []
    for o in range(1, columns):
        copy = pltpu.make_async_remote_copy(
            src_ref=dev_buf.at[d], dst_ref=dev_buf.at[d],
            send_sem=dev_send.at[o], recv_sem=dev_recv.at[d],
            device_id=(g, lax.rem(d + o, columns)), device_id_type=MESH,
        )
        copy.start()
        copies.append(copy)
    for o in range(1, columns):
        source = lax.rem(d + columns - o, columns)
        pltpu.make_async_remote_copy(
            src_ref=dev_buf.at[source], dst_ref=dev_buf.at[source],
            send_sem=dev_send.at[o], recv_sem=dev_recv.at[source],
            device_id=(g, source), device_id_type=MESH,
        ).wait_recv()
    for copy in copies:
        copy.wait_send()
    packed = jnp.sum(dev_buf[...], axis=0)
    full = jnp.concatenate([packed, pltpu.roll(packed, LANES // 2, 1)], axis=0)
    coef = full[:, 0:rank] / full[:, rank:rank + 1]
    high = coef.astype(jnp.bfloat16)
    rest = coef - high.astype(jnp.float32)
    middle = rest.astype(jnp.bfloat16)
    low = (rest - middle.astype(jnp.float32)).astype(jnp.bfloat16)
    basis = basis_ref[...]
    shade = (
        jnp.dot(low, basis, preferred_element_type=jnp.float32)
        + jnp.dot(middle, basis, preferred_element_type=jnp.float32)
        + jnp.dot(high, basis, preferred_element_type=jnp.float32)
    )
    inverse = jnp.exp(-shade)
    dark = dark_ref[...].astype(jnp.float32)
    plane = lax.broadcasted_iota(jnp.int32, (planes, pixels), 0)
    for t in range(tiles):
        fixed = (raw_ref[t].astype(jnp.float32) - dark) * inverse
        corrected_ref[t] = jnp.where(plane < counts_ref[t], fixed, 0.0).astype(jnp.bfloat16)

    pieces = []
    for block in range(blocks):
        kind = 0 if block == 0 else 2 if block == blocks - 1 else 1
        total = None
        for row in range(ROWS):
            start = row * COLS + block * BLOCK
            part = jnp.dot(
                corrected_ref[:, :, start:start + BLOCK].reshape(tiles * planes, BLOCK),
                weights[kind],
                preferred_element_type=jnp.float32,
            )
            total = part if total is None else total + part
        pieces.append(total)
    cells = jnp.concatenate(pieces, axis=1)

    mine = (g * columns + d) * tiles
    place = [positions_ref[mine + t] for t in range(tiles)]
    for b in range(groups):
        chosen = jnp.zeros((planes, cells_wide), jnp.float32)
        tail = jnp.zeros((planes, LANES), jnp.float32)
        for t in range(tiles):
            rows = cells[t * planes:(t + 1) * planes]
            band = jnp.full((planes, cells_wide), lax.div(place[t], band_size), jnp.int32)
            chosen = jnp.where(band == b, rows, chosen)
            ends = jnp.full((planes, LANES), place[t], jnp.int32)
            final = jnp.full((planes, LANES), lax.rem(place[t], tiles), jnp.int32)
            hit = (ends >= b * band_size) & (ends < (b + 1) * band_size) & (final == tiles - 1)
            tail = jnp.where(hit, rows[:, last:], tail)
        outgoing[b] = chosen.astype(jnp.bfloat16)
        tail_out[b] = tail.astype(jnp.bfloat16)

    def cell_copy(o):
        other = lax.rem(g + o, groups)
        return pltpu.make_async_remote_copy(
            src_ref=outgoing.at[other], dst_ref=arrived.at[g],
            send_sem=cell_send.at[o], recv_sem=cell_recv.at[g],
            device_id=(other, d), device_id_type=MESH,
        )

    def tail_copy(o):
        other = lax.rem(g + o, groups)
        return pltpu.make_async_remote_copy(
            src_ref=tail_out.at[other], dst_ref=tail_in.at[g],
            send_sem=tail_send.at[o], recv_sem=tail_recv.at[g],
            device_id=(other, lax.rem(d + 1, columns)), device_id_type=MESH,
        )

    for o in range(1, groups):
        cell_copy(o).start()

    @pl.when(d < columns - 1)
    def _():
        for o in range(groups):
            tail_copy(o).start()

    acc[...] = jnp.zeros_like(acc)
    arrived[g] = outgoing[g]
    for o in range(1, groups):
        source = lax.rem(g + groups - o, groups)
        pltpu.make_async_remote_copy(
            src_ref=outgoing.at[source], dst_ref=arrived.at[source],
            send_sem=cell_send.at[o], recv_sem=cell_recv.at[source],
            device_id=(source, d), device_id_type=MESH,
        ).wait_recv()
    slots = []
    for source in range(groups):
        slot = jnp.int32(0)
        for t in range(tiles):
            at = positions_ref[(source * columns + d) * tiles + t]
            slot = slot + jnp.where(lax.div(at, band_size) == g, lax.rem(at, tiles), 0)
        slots.append(slot)
    for j in range(tiles):
        cell = jnp.zeros((planes, cells_wide), jnp.float32)
        for source in range(groups):
            here = jnp.full((planes, cells_wide), slots[source], jnp.int32) == j
            cell = jnp.where(here, arrived[source].astype(jnp.float32), cell)
        base, shift = divmod(j * half_step, LANES)
        base = base * LANES
        if shift:
            cell = jnp.concatenate([cell, jnp.zeros((planes, LANES), jnp.float32)], axis=1)
            cell = pltpu.roll(cell, shift, 1)
        acc[:, base:base + cell.shape[1]] += cell

    @pl.when(d > 0)
    def _():
        spill = jnp.zeros((planes, LANES), jnp.float32)
        for o in range(groups):
            source = lax.rem(g + groups - o, groups)
            pltpu.make_async_remote_copy(
                src_ref=tail_out.at[source], dst_ref=tail_in.at[source],
                send_sem=tail_send.at[o], recv_sem=tail_recv.at[source],
                device_id=(source, lax.rem(d + columns - 1, columns)), device_id_type=MESH,
            ).wait_recv()
        for source in range(groups):
            spill = spill + tail_in[source].astype(jnp.float32)
        spill = pltpu.roll(spill, half_ovl, 1)
        lane = lax.broadcasted_iota(jnp.int32, (planes, LANES), 1)
        acc[:, 0:LANES] += jnp.where(lane < half_ovl, spill, 0.0)

    pooled_ref[...] = acc[:, 0:tiles * half_step].astype(jnp.bfloat16)
    for o in range(1, groups):
        cell_copy(o).wait_send()

    @pl.when(d < columns - 1)
    def _():
        for o in range(groups):
            tail_copy(o).wait_send()


def per_device(groups, columns, raw, dark, basis, counts, positions):
    tiles, planes, pixels = raw.shape
    half_step = (COLS - OVL) // 2
    bf16, f32 = jnp.bfloat16, jnp.float32
    vmem = pl.BlockSpec(memory_space=pltpu.VMEM)
    smem = pl.BlockSpec(memory_space=pltpu.SMEM)
    dma = pltpu.SemaphoreType.DMA
    corrected, pooled = pl.pallas_call(
        functools.partial(kernel, groups, columns),
        out_shape=(
            jax.ShapeDtypeStruct(raw.shape, bf16),
            jax.ShapeDtypeStruct((planes, tiles * half_step), bf16),
        ),
        in_specs=[smem, smem, vmem, vmem, vmem],
        out_specs=(vmem, vmem),
        scratch_shapes=[
            pltpu.VMEM((16, pixels), bf16),
            pltpu.VMEM((planes, LANES), f32),
            pltpu.VMEM((groups, planes // 2, LANES), f32),
            pltpu.VMEM((columns, planes // 2, LANES), f32),
            pltpu.VMEM((3, BLOCK, LANES), bf16),
            pltpu.VMEM((groups, planes, COLS // 2), bf16),
            pltpu.VMEM((groups, planes, COLS // 2), bf16),
            pltpu.VMEM((groups, planes, LANES), bf16),
            pltpu.VMEM((groups, planes, LANES), bf16),
            pltpu.VMEM((planes, tiles * half_step + LANES), f32),
            dma((groups,)), dma((groups,)), dma((columns,)), dma((columns,)),
            dma((groups,)), dma((groups,)), dma((groups,)), dma((groups,)),
        ],
        compiler_params=pltpu.CompilerParams(collective_id=0, has_side_effects=True),
    )(counts, positions, raw, dark, basis)
    return corrected, pooled.reshape(1, planes, ROWS // 2, tiles * half_step)


def solution(mesh):
    in_specs = (P(("grp", "dev"), None, None), P(), P(), P(("grp", "dev")), P())
    out_specs = (P(("grp", "dev"), None, None), P("grp", None, None, "dev"))
    return jax.shard_map(
        functools.partial(per_device, mesh.shape["grp"], mesh.shape["dev"]),
        mesh=mesh, in_specs=in_specs, out_specs=out_specs, check_vma=False,
    )
```

time: 95.3 us -> 22.4 us (0.24)
  the two profiles are of different devices: /device:TPU:1 before, /device:TPU:0 now
where the time goes in v1:
time: 22.4 us; the launch traced here: 22.2 us
  Pallas kernels  19 us (85%)
  local copies, waits for them, and re-layouts  2.56 us (11%)
  between operations  0.65 us (3%)
    pallas_call x1, Pallas kernels, per_device(): pl.pallas_call(functools.partial(kernel, groups, columns), out_shape=(jax...  19 us
    unnamed x4, local copies, waits for them, and re-layouts  2.56 us

profile of v1, /device:TPU:0, one launch (start us, length us, event | category | flops | bytes accessed | tf_op | source)
XLA Modules:
  0.0 22.2 jit_solution(1728965315303971460)
XLA Ops:
  0.6 19.0 %shard_map.68 = (bf16[4,16,4096]{2,1,0:T(8,128)(2,1)}, bf16[16,3840]{1,0:T(8,128)(2,1)}) custom-call(s32[4]{0:T(128)} %counts_ref.1, s32[128]{0:T(128)} %positions_ref.1, bf16[4,16,4096]{2,1,0:T(8,128)(2,1)} %raw_ref.1, bf16[16,4096]{1,0:T(8,128)(2,1)} %dark_ref.1, bf16[8,4096]{1,0:T(8,128)(2,1)} %basis_ref.1), custom_call_target="tpu_custom_call" | custom-call | tf_op jit(solution)/shard_map/pallas_call | solution.py:254
  19.6 0.0 copy-start
  19.7 1.9 %copy.9 = bf16[4,16,4096]{2,1,0:T(8,128)(2,1)} copy(bf16[4,16,4096]{2,1,0:T(8,128)(2,1)} %get-tuple-element.8) | data formatting | bytes 1048576
  21.6 0.0 copy-done
  21.6 0.6 %copy.10 = bf16[1,16,1,3840]{3,1,2,0:T(8,128)(2,1)} copy(bf16[1,16,1,3840]{3,1,2,0:T(8,128)(2,1)S(1)} %bitcast.1) | data formatting | bytes 245760
Async XLA Ops:
  19.6 1.9 %copy-start = (bf16[16,3840]{1,0:T(8,128)(2,1)S(1)}, bf16[16,3840]{1,0:T(8,128)(2,1)}, u32[]{:S(2)}) copy-start(bf16[16,3840]{1,0:T(8,128)(2,1)} %get-tuple-element.5) | copy-start | bytes 368644

commit v2 on v1

--- a/solution.py
+++ b/solution.py
@@ -27,21 +27,34 @@
 
 def kernel(
     groups, columns,
-    counts_ref, positions_ref, raw_ref, dark_ref, basis_ref,
-    corrected_ref, pooled_ref,
-    rhs, stat, grp_buf, dev_buf, weights, outgoing, arrived, tail_out, tail_in, acc,
+    counts_hbm, positions_hbm, raw_hbm, dark_hbm, basis_hbm,
+    corrected_hbm, pooled_ref,
+    counts_ref, positions_ref, raw_ref, dark_ref, rhs, corrected_ref,
+    stat, grp_buf, dev_buf, weights, outgoing, arrived, tail_out, tail_in, acc,
+    in_sem, raw_sem, out_sem,
     grp_send, grp_recv, dev_send, dev_recv, cell_send, cell_recv, tail_send, tail_recv,
 ):
     tiles, planes, pixels = raw_ref.shape
-    rank = basis_ref.shape[0]
+    rank = basis_hbm.shape[0]
     band_size = columns * tiles
     half_step = (COLS - OVL) // 2
     half_ovl = OVL // 2
     cells_wide = COLS // 2
-    last = cells_wide - LANES
     blocks = COLS // BLOCK
     g = lax.axis_index("grp")
     d = lax.axis_index("dev")
+
+    raw_loads = [
+        pltpu.make_async_copy(raw_hbm.at[t], raw_ref.at[t], raw_sem.at[t]) for t in range(tiles)
+    ]
+    loads = [
+        pltpu.make_async_copy(basis_hbm, rhs.at[0:rank], in_sem.at[0]),
+        pltpu.make_async_copy(dark_hbm, dark_ref, in_sem.at[1]),
+        pltpu.make_async_copy(counts_hbm, counts_ref, in_sem.at[2]),
+        pltpu.make_async_copy(positions_hbm, positions_ref, in_sem.at[3]),
+    ]
+    for copy in loads[:2] + raw_loads + loads[2:]:
+        copy.start()
 
     barrier = pltpu.get_barrier_semaphore()
     near = [lax.rem(d + 1, columns), lax.rem(d + columns - 1, columns)]
@@ -54,27 +67,33 @@
             barrier, inc=1, device_id=(g, lax.rem(d + o, columns)), device_id_type=MESH
         )
 
-    rhs[0:rank, :] = basis_ref[...]
     rhs[rank:, :] = jnp.ones((rhs.shape[0] - rank, pixels), jnp.bfloat16)
     width = rhs.shape[0]
+    weights[0] = pool_weights(0, blocks)
+    weights[1] = pool_weights(1, blocks)
+    weights[2] = pool_weights(blocks - 1, blocks)
+    stat[...] = jnp.zeros_like(stat)
+    for copy in loads:
+        copy.wait()
+    dark_sums = lax.dot_general(dark_ref[...], rhs[...], NT, preferred_element_type=jnp.float32)
+    plane = lax.broadcasted_iota(jnp.int32, (planes, width), 0)
+    for copy in raw_loads:
+        copy.wait()
     sums = lax.dot_general(
         raw_ref[...].reshape(tiles * planes, pixels), rhs[...], NT,
         preferred_element_type=jnp.float32,
     )
-    dark_sums = lax.dot_general(dark_ref[...], rhs[...], NT, preferred_element_type=jnp.float32)
-    plane = lax.broadcasted_iota(jnp.int32, (planes, width), 0)
     local = jnp.zeros((planes, width), jnp.float32)
     for t in range(tiles):
         part = sums[t * planes:(t + 1) * planes] - dark_sums
         local = local + jnp.where(plane < counts_ref[t], part, 0.0)
-    stat[...] = jnp.zeros_like(stat)
     stat[:, 0:width] = local
     half = planes // 2
     grp_buf[g] = stat[0:half, :] + pltpu.roll(stat[half:, :], LANES // 2, 1)
 
     pl.semaphore_wait(barrier, 3 * (groups - 1) + columns - 1)
 
-    copies = []
+    sent = []
     for o in range(1, groups):
         other = lax.rem(g + o, groups)
         copy = pltpu.make_async_remote_copy(
@@ -83,10 +102,7 @@
             device_id=(other, d), device_id_type=MESH,
         )
         copy.start()
-        copies.append(copy)
-    weights[0] = pool_weights(0, blocks)
-    weights[1] = pool_weights(1, blocks)
-    weights[2] = pool_weights(blocks - 1, blocks)
+        sent.append(copy)
     for o in range(1, groups):
         source = lax.rem(g + groups - o, groups)
         pltpu.make_async_remote_copy(
@@ -94,10 +110,7 @@
             send_sem=grp_send.at[o], recv_sem=grp_recv.at[source],
             device_id=(source, d), device_id_type=MESH,
         ).wait_recv()
-    for copy in copies:
-        copy.wait_send()
     dev_buf[d] = jnp.sum(grp_buf[...], axis=0)
-    copies = []
     for o in range(1, columns):
         copy = pltpu.make_async_remote_copy(
             src_ref=dev_buf.at[d], dst_ref=dev_buf.at[d],
@@ -105,7 +118,8 @@
             device_id=(g, lax.rem(d + o, columns)), device_id_type=MESH,
         )
         copy.start()
-        copies.append(copy)
+        sent.append(copy)
+    acc[...] = jnp.zeros_like(acc)
     for o in range(1, columns):
         source = lax.rem(d + columns - o, columns)
         pltpu.make_async_remote_copy(
@@ -113,8 +127,6 @@
             send_sem=dev_send.at[o], recv_sem=dev_recv.at[source],
             device_id=(g, source), device_id_type=MESH,
         ).wait_recv()
-    for copy in copies:
-        copy.wait_send()
     packed = jnp.sum(dev_buf[...], axis=0)
     full = jnp.concatenate([packed, pltpu.roll(packed, LANES // 2, 1)], axis=0)
     coef = full[:, 0:rank] / full[:, rank:rank + 1]
@@ -122,49 +134,49 @@
     rest = coef - high.astype(jnp.float32)
     middle = rest.astype(jnp.bfloat16)
     low = (rest - middle.astype(jnp.float32)).astype(jnp.bfloat16)
-    basis = basis_ref[...]
-    shade = (
-        jnp.dot(low, basis, preferred_element_type=jnp.float32)
-        + jnp.dot(middle, basis, preferred_element_type=jnp.float32)
-        + jnp.dot(high, basis, preferred_element_type=jnp.float32)
-    )
-    inverse = jnp.exp(-shade)
-    dark = dark_ref[...].astype(jnp.float32)
-    plane = lax.broadcasted_iota(jnp.int32, (planes, pixels), 0)
-    for t in range(tiles):
-        fixed = (raw_ref[t].astype(jnp.float32) - dark) * inverse
-        corrected_ref[t] = jnp.where(plane < counts_ref[t], fixed, 0.0).astype(jnp.bfloat16)
-
-    pieces = []
+
+    mine = (g * columns + d) * tiles
+    place = [positions_ref[mine + t] for t in range(tiles)]
+    band_of = [jnp.full((planes, LANES), lax.div(p, band_size), jnp.int32) for p in place]
+    slot_of = [jnp.full((planes, LANES), lax.rem(p, tiles), jnp.int32) for p in place]
+    plane = lax.broadcasted_iota(jnp.int32, (planes, BLOCK), 0)
+    live = [plane < counts_ref[t] for t in range(tiles)]
     for block in range(blocks):
         kind = 0 if block == 0 else 2 if block == blocks - 1 else 1
         total = None
         for row in range(ROWS):
-            start = row * COLS + block * BLOCK
+            span = slice(row * COLS + block * BLOCK, row * COLS + (block + 1) * BLOCK)
+            basis = rhs[0:rank, span]
+            shade = (
+                jnp.dot(low, basis, preferred_element_type=jnp.float32)
+                + jnp.dot(middle, basis, preferred_element_type=jnp.float32)
+                + jnp.dot(high, basis, preferred_element_type=jnp.float32)
+            )
+            inverse = jnp.exp(-shade)
+            dark = dark_ref[:, span].astype(jnp.float32)
+            made = []
+            for t in range(tiles):
+                fixed = (raw_ref[t, :, span].astype(jnp.float32) - dark) * inverse
+                fixed = jnp.where(live[t], fixed, 0.0).astype(jnp.bfloat16)
+                corrected_ref[t, :, span] = fixed
+                made.append(fixed)
             part = jnp.dot(
-                corrected_ref[:, :, start:start + BLOCK].reshape(tiles * planes, BLOCK),
-                weights[kind],
-                preferred_element_type=jnp.float32,
+                jnp.concatenate(made, axis=0), weights[kind], preferred_element_type=jnp.float32
             )
             total = part if total is None else total + part
-        pieces.append(total)
-    cells = jnp.concatenate(pieces, axis=1)
-
-    mine = (g * columns + d) * tiles
-    place = [positions_ref[mine + t] for t in range(tiles)]
-    for b in range(groups):
-        chosen = jnp.zeros((planes, cells_wide), jnp.float32)
-        tail = jnp.zeros((planes, LANES), jnp.float32)
-        for t in range(tiles):
-            rows = cells[t * planes:(t + 1) * planes]
-            band = jnp.full((planes, cells_wide), lax.div(place[t], band_size), jnp.int32)
-            chosen = jnp.where(band == b, rows, chosen)
-            ends = jnp.full((planes, LANES), place[t], jnp.int32)
-            final = jnp.full((planes, LANES), lax.rem(place[t], tiles), jnp.int32)
-            hit = (ends >= b * band_size) & (ends < (b + 1) * band_size) & (final == tiles - 1)
-            tail = jnp.where(hit, rows[:, last:], tail)
-        outgoing[b] = chosen.astype(jnp.bfloat16)
-        tail_out[b] = tail.astype(jnp.bfloat16)
+        lanes = slice(block * LANES, (block + 1) * LANES)
+        rows = [total[t * planes:(t + 1) * planes] for t in range(tiles)]
+        for b in range(groups):
+            chosen = jnp.zeros((planes, LANES), jnp.float32)
+            tail = jnp.zeros((planes, LANES), jnp.float32)
+            for t in range(tiles):
+                hit = band_of[t] == b
+                chosen = jnp.where(hit, rows[t], chosen)
+                if block == blocks - 1:
+                    tail = jnp.where(hit & (slot_of[t] == tiles - 1), rows[t], tail)
+            outgoing[b, :, lanes] = chosen.astype(jnp.bfloat16)
+            if block == blocks - 1:
+                tail_out[b] = tail.astype(jnp.bfloat16)
 
     def cell_copy(o):
         other = lax.rem(g + o, groups)
@@ -190,7 +202,12 @@
         for o in range(groups):
             tail_copy(o).start()
 
-    acc[...] = jnp.zeros_like(acc)
+    stores = [
+        pltpu.make_async_copy(corrected_ref.at[t], corrected_hbm.at[t], out_sem.at[t])
+        for t in range(tiles)
+    ]
+    for copy in stores:
+        copy.start()
     arrived[g] = outgoing[g]
     for o in range(1, groups):
         source = lax.rem(g + groups - o, groups)
@@ -235,6 +252,10 @@
         acc[:, 0:LANES] += jnp.where(lane < half_ovl, spill, 0.0)
 
     pooled_ref[...] = acc[:, 0:tiles * half_step].astype(jnp.bfloat16)
+    for copy in sent:
+        copy.wait_send()
+    for copy in stores:
+        copy.wait()
     for o in range(1, groups):
         cell_copy(o).wait_send()
 
@@ -249,7 +270,7 @@
     half_step = (COLS - OVL) // 2
     bf16, f32 = jnp.bfloat16, jnp.float32
     vmem = pl.BlockSpec(memory_space=pltpu.VMEM)
-    smem = pl.BlockSpec(memory_space=pltpu.SMEM)
+    anywhere = pl.BlockSpec(memory_space=pl.ANY)
     dma = pltpu.SemaphoreType.DMA
     corrected, pooled = pl.pallas_call(
         functools.partial(kernel, groups, columns),
@@ -257,10 +278,15 @@
             jax.ShapeDtypeStruct(raw.shape, bf16),
             jax.ShapeDtypeStruct((planes, tiles * half_step), bf16),
         ),
-        in_specs=[smem, smem, vmem, vmem, vmem],
-        out_specs=(vmem, vmem),
+        in_specs=[anywhere] * 5,
+        out_specs=(anywhere, vmem),
         scratch_shapes=[
+            pltpu.SMEM(counts.shape, jnp.int32),
+            pltpu.SMEM(positions.shape, jnp.int32),
+            pltpu.VMEM(raw.shape, bf16),
+            pltpu.VMEM(dark.shape, bf16),
             pltpu.VMEM((16, pixels), bf16),
+            pltpu.VMEM(raw.shape, bf16),
             pltpu.VMEM((planes, LANES), f32),
             pltpu.VMEM((groups, planes // 2, LANES), f32),
             pltpu.VMEM((columns, planes // 2, LANES), f32),
@@ -270,11 +296,14 @@
             pltpu.VMEM((groups, planes, LANES), bf16),
             pltpu.VMEM((groups, planes, LANES), bf16),
             pltpu.VMEM((planes, tiles * half_step + LANES), f32),
+            dma((4,)), dma((tiles,)), dma((tiles,)),
             dma((groups,)), dma((groups,)), dma((columns,)), dma((columns,)),
             dma((groups,)), dma((groups,)), dma((groups,)), dma((groups,)),
         ],
-        compiler_params=pltpu.CompilerParams(collective_id=0, has_side_effects=True),
-    )(counts, positions, raw, dark, basis)
+        compiler_params=pltpu.CompilerParams(
+            collective_id=0, has_side_effects=True, vmem_limit_bytes=16 << 20
+        ),
+    )(*[pltpu.with_memory_space_constraint(x, pltpu.HBM) for x in (counts, positions, raw, dark, basis)])
     return corrected, pooled.reshape(1, planes, ROWS // 2, tiles * half_step)
 
 

time: 22.4 us -> 20.2 us (0.902)
  local copies, waits for them, and re-layouts: 2.56 us -> 1.44 us
  Pallas kernels: 19 us -> 18 us
    unnamed x4 -> x2, local copies, waits for them, and re-layouts: 2.56 us -> 1.44 us
    pallas_call x1, Pallas kernels: 19 us -> 18 us  [per_device(): pl.pallas_call(functools.partial(kernel, groups, columns), out_shape=(jax...]
where the time goes in v2:
time: 20.2 us; the launch traced here: 20.1 us
  Pallas kernels  18 us (89%)
  local copies, waits for them, and re-layouts  1.44 us (7%)
  between operations  0.64 us (3%)
    pallas_call x1, Pallas kernels, per_device(): pl.pallas_call(functools.partial(kernel, groups, columns), out_shape=(jax...  18 us
    unnamed x2, local copies, waits for them, and re-layouts  1.44 us

profile of v2, /device:TPU:0, one launch (start us, length us, event | category | flops | bytes accessed | tf_op | source)
XLA Modules:
  0.0 20.1 jit_solution(604233552645203111)
XLA Ops:
  0.6 18.0 %shard_map.68 = (bf16[4,16,4096]{2,1,0:T(8,128)(2,1)S(1)}, bf16[16,3840]{1,0:T(8,128)(2,1)S(1)}) custom-call(s32[4]{0:T(128)} %counts_hbm.1, s32[128]{0:T(128)} %positions_hbm.1, bf16[4,16,4096]{2,1,0:T(8,128)(2,1)} %raw_hbm.1, bf16[16,4096]{1,0:T(8,128)(2,1)} %dark_hbm.1, bf16[8,4096]{1,0:T(8,128)(2,1)} %basis_hbm.1), custom_call_target="tpu_custom_call" | custom-call | tf_op jit(solution)/shard_map/pallas_call | solution.py:275
  18.7 0.8 %copy.9 = bf16[4,16,4096]{2,1,0:T(8,128)(2,1)} copy(bf16[4,16,4096]{2,1,0:T(8,128)(2,1)S(1)} %get-tuple-element.8) | data formatting | bytes 1048576
  19.5 0.6 %copy.10 = bf16[1,16,1,3840]{3,1,2,0:T(8,128)(2,1)} copy(bf16[1,16,1,3840]{3,1,2,0:T(8,128)(2,1)S(1)} %bitcast.1) | data formatting | bytes 245760

commit v3 on v2

--- a/solution.py
+++ b/solution.py
@@ -16,6 +16,13 @@
 NT = (((1,), (1,)), ((), ()))
 
 
+def pick(options):
+    found = jnp.int32(0)
+    for hit, value in options:
+        found = jnp.where(hit, value, found)
+    return found
+
+
 def pool_weights(block, blocks):
     row = lax.broadcasted_iota(jnp.int32, (BLOCK, LANES), 0)
     lane = lax.broadcasted_iota(jnp.int32, (BLOCK, LANES), 1)
@@ -30,7 +37,7 @@
     counts_hbm, positions_hbm, raw_hbm, dark_hbm, basis_hbm,
     corrected_hbm, pooled_ref,
     counts_ref, positions_ref, raw_ref, dark_ref, rhs, corrected_ref,
-    stat, grp_buf, dev_buf, weights, outgoing, arrived, tail_out, tail_in, acc,
+    stat, grp_buf, dev_buf, weights, outgoing, arrived, tail_out, tail_in, inverse_ref, placed, acc,
     in_sem, raw_sem, out_sem,
     grp_send, grp_recv, dev_send, dev_recv, cell_send, cell_recv, tail_send, tail_recv,
 ):
@@ -39,7 +46,6 @@
     band_size = columns * tiles
     half_step = (COLS - OVL) // 2
     half_ovl = OVL // 2
-    cells_wide = COLS // 2
     blocks = COLS // BLOCK
     g = lax.axis_index("grp")
     d = lax.axis_index("dev")
@@ -91,6 +97,22 @@
     half = planes // 2
     grp_buf[g] = stat[0:half, :] + pltpu.roll(stat[half:, :], LANES // 2, 1)
 
+    def home(at):
+        return lax.div(at, band_size), lax.rem(at, tiles)
+
+    wide = lax.broadcasted_iota(jnp.int32, (planes, pixels), 0)
+    mine = [home(positions_ref[(g * columns + d) * tiles + t]) for t in range(tiles)]
+    for b in range(groups):
+        chosen = pick((mine[t][0] == b, t) for t in range(tiles))
+        masked = jnp.where(
+            wide < counts_ref[chosen],
+            raw_ref[chosen].astype(jnp.float32), dark_ref[...].astype(jnp.float32),
+        ).astype(jnp.bfloat16)
+        outgoing[b] = masked
+        for row in range(ROWS):
+            tail_out[b, row] = masked[:, (row + 1) * COLS - OVL:(row + 1) * COLS]
+    arrived[g] = outgoing[g]
+
     pl.semaphore_wait(barrier, 3 * (groups - 1) + columns - 1)
 
     sent = []
@@ -103,6 +125,31 @@
         )
         copy.start()
         sent.append(copy)
+
+    def cell_copy(o):
+        other = lax.rem(g + o, groups)
+        return pltpu.make_async_remote_copy(
+            src_ref=outgoing.at[other], dst_ref=arrived.at[g],
+            send_sem=cell_send.at[o], recv_sem=cell_recv.at[g],
+            device_id=(other, d), device_id_type=MESH,
+        )
+
+    def tail_copy(o):
+        other = lax.rem(g + o, groups)
+        return pltpu.make_async_remote_copy(
+            src_ref=tail_out.at[other], dst_ref=tail_in.at[g],
+            send_sem=tail_send.at[o], recv_sem=tail_recv.at[g],
+            device_id=(other, lax.rem(d + 1, columns)), device_id_type=MESH,
+        )
+
+    @pl.when(d < columns - 1)
+    def _():
+        for o in range(groups):
+            tail_copy(o).start()
+
+    for o in range(1, groups):
+        cell_copy(o).start()
+
     for o in range(1, groups):
         source = lax.rem(g + groups - o, groups)
         pltpu.make_async_remote_copy(
@@ -135,72 +182,22 @@
     middle = rest.astype(jnp.bfloat16)
     low = (rest - middle.astype(jnp.float32)).astype(jnp.bfloat16)
 
-    mine = (g * columns + d) * tiles
-    place = [positions_ref[mine + t] for t in range(tiles)]
-    band_of = [jnp.full((planes, LANES), lax.div(p, band_size), jnp.int32) for p in place]
-    slot_of = [jnp.full((planes, LANES), lax.rem(p, tiles), jnp.int32) for p in place]
+    parts = jnp.concatenate([low, middle, high], axis=1)
     plane = lax.broadcasted_iota(jnp.int32, (planes, BLOCK), 0)
     live = [plane < counts_ref[t] for t in range(tiles)]
-    for block in range(blocks):
-        kind = 0 if block == 0 else 2 if block == blocks - 1 else 1
-        total = None
-        for row in range(ROWS):
-            span = slice(row * COLS + block * BLOCK, row * COLS + (block + 1) * BLOCK)
-            basis = rhs[0:rank, span]
-            shade = (
-                jnp.dot(low, basis, preferred_element_type=jnp.float32)
-                + jnp.dot(middle, basis, preferred_element_type=jnp.float32)
-                + jnp.dot(high, basis, preferred_element_type=jnp.float32)
-            )
-            inverse = jnp.exp(-shade)
-            dark = dark_ref[:, span].astype(jnp.float32)
-            made = []
-            for t in range(tiles):
-                fixed = (raw_ref[t, :, span].astype(jnp.float32) - dark) * inverse
-                fixed = jnp.where(live[t], fixed, 0.0).astype(jnp.bfloat16)
-                corrected_ref[t, :, span] = fixed
-                made.append(fixed)
-            part = jnp.dot(
-                jnp.concatenate(made, axis=0), weights[kind], preferred_element_type=jnp.float32
-            )
-            total = part if total is None else total + part
-        lanes = slice(block * LANES, (block + 1) * LANES)
-        rows = [total[t * planes:(t + 1) * planes] for t in range(tiles)]
-        for b in range(groups):
-            chosen = jnp.zeros((planes, LANES), jnp.float32)
-            tail = jnp.zeros((planes, LANES), jnp.float32)
-            for t in range(tiles):
-                hit = band_of[t] == b
-                chosen = jnp.where(hit, rows[t], chosen)
-                if block == blocks - 1:
-                    tail = jnp.where(hit & (slot_of[t] == tiles - 1), rows[t], tail)
-            outgoing[b, :, lanes] = chosen.astype(jnp.bfloat16)
-            if block == blocks - 1:
-                tail_out[b] = tail.astype(jnp.bfloat16)
-
-    def cell_copy(o):
-        other = lax.rem(g + o, groups)
-        return pltpu.make_async_remote_copy(
-            src_ref=outgoing.at[other], dst_ref=arrived.at[g],
-            send_sem=cell_send.at[o], recv_sem=cell_recv.at[g],
-            device_id=(other, d), device_id_type=MESH,
-        )
-
-    def tail_copy(o):
-        other = lax.rem(g + o, groups)
-        return pltpu.make_async_remote_copy(
-            src_ref=tail_out.at[other], dst_ref=tail_in.at[g],
-            send_sem=tail_send.at[o], recv_sem=tail_recv.at[g],
-            device_id=(other, lax.rem(d + 1, columns)), device_id_type=MESH,
-        )
-
-    for o in range(1, groups):
-        cell_copy(o).start()
-
-    @pl.when(d < columns - 1)
-    def _():
-        for o in range(groups):
-            tail_copy(o).start()
+    for block in range(pixels // BLOCK):
+        span = slice(block * BLOCK, (block + 1) * BLOCK)
+        basis = rhs[0:rank, span]
+        shade = jnp.dot(
+            parts, jnp.concatenate([basis, basis, basis], axis=0),
+            preferred_element_type=jnp.float32,
+        )
+        inverse = jnp.exp(-shade)
+        inverse_ref[:, span] = inverse
+        dark = dark_ref[:, span].astype(jnp.float32)
+        for t in range(tiles):
+            fixed = (raw_ref[t, :, span].astype(jnp.float32) - dark) * inverse
+            corrected_ref[t, :, span] = jnp.where(live[t], fixed, 0.0).astype(jnp.bfloat16)
 
     stores = [
         pltpu.make_async_copy(corrected_ref.at[t], corrected_hbm.at[t], out_sem.at[t])
@@ -208,7 +205,6 @@
     ]
     for copy in stores:
         copy.start()
-    arrived[g] = outgoing[g]
     for o in range(1, groups):
         source = lax.rem(g + groups - o, groups)
         pltpu.make_async_remote_copy(
@@ -216,18 +212,37 @@
             send_sem=cell_send.at[o], recv_sem=cell_recv.at[source],
             device_id=(source, d), device_id_type=MESH,
         ).wait_recv()
-    slots = []
-    for source in range(groups):
-        slot = jnp.int32(0)
-        for t in range(tiles):
-            at = positions_ref[(source * columns + d) * tiles + t]
-            slot = slot + jnp.where(lax.div(at, band_size) == g, lax.rem(at, tiles), 0)
-        slots.append(slot)
+    there = [
+        [home(positions_ref[(s * columns + d) * tiles + t]) for t in range(tiles)]
+        for s in range(groups)
+    ]
+    slots = [
+        pick((band == g, slot) for band, slot in there[s]) for s in range(groups)
+    ]
+    origin = [
+        pick((slots[s] == j, s) for s in range(groups)) for j in range(tiles)
+    ]
+    for block in range(blocks):
+        kind = 0 if block == 0 else 2 if block == blocks - 1 else 1
+        total = None
+        for row in range(ROWS):
+            span = slice(row * COLS + block * BLOCK, row * COLS + (block + 1) * BLOCK)
+            dark = dark_ref[:, span].astype(jnp.float32)
+            inverse = inverse_ref[:, span]
+            made = [
+                ((arrived[origin[j], :, span].astype(jnp.float32) - dark) * inverse)
+                .astype(jnp.bfloat16) for j in range(tiles)
+            ]
+            part = jnp.dot(
+                jnp.concatenate(made, axis=0), weights[kind], preferred_element_type=jnp.float32
+            )
+            total = part if total is None else total + part
+        lanes = slice(block * LANES, (block + 1) * LANES)
+        total = total.astype(jnp.bfloat16).astype(jnp.float32)
+        for j in range(tiles):
+            placed[j, :, lanes] = total[j * planes:(j + 1) * planes]
     for j in range(tiles):
-        cell = jnp.zeros((planes, cells_wide), jnp.float32)
-        for source in range(groups):
-            here = jnp.full((planes, cells_wide), slots[source], jnp.int32) == j
-            cell = jnp.where(here, arrived[source].astype(jnp.float32), cell)
+        cell = placed[j]
         base, shift = divmod(j * half_step, LANES)
         base = base * LANES
         if shift:
@@ -245,8 +260,24 @@
                 send_sem=tail_send.at[o], recv_sem=tail_recv.at[source],
                 device_id=(source, lax.rem(d + columns - 1, columns)), device_id_type=MESH,
             ).wait_recv()
-        for source in range(groups):
-            spill = spill + tail_in[source].astype(jnp.float32)
+        before = [
+            [home(positions_ref[(s * columns + d - 1) * tiles + t]) for t in range(tiles)]
+            for s in range(groups)
+        ]
+        final = pick(
+            ((band == g) & (slot == tiles - 1), s)
+            for s in range(groups) for band, slot in before[s]
+        )
+        for row in range(ROWS):
+            span = slice((row + 1) * COLS - OVL, (row + 1) * COLS)
+            fixed = (
+                (tail_in[final, row].astype(jnp.float32) - dark_ref[:, span].astype(jnp.float32))
+                * inverse_ref[:, span]
+            ).astype(jnp.bfloat16)
+            spill = spill + jnp.dot(
+                fixed, weights[2, BLOCK - OVL:, :], preferred_element_type=jnp.float32
+            )
+        spill = spill.astype(jnp.bfloat16).astype(jnp.float32)
         spill = pltpu.roll(spill, half_ovl, 1)
         lane = lax.broadcasted_iota(jnp.int32, (planes, LANES), 1)
         acc[:, 0:LANES] += jnp.where(lane < half_ovl, spill, 0.0)
@@ -291,10 +322,12 @@
             pltpu.VMEM((groups, planes // 2, LANES), f32),
             pltpu.VMEM((columns, planes // 2, LANES), f32),
             pltpu.VMEM((3, BLOCK, LANES), bf16),
-            pltpu.VMEM((groups, planes, COLS // 2), bf16),
-            pltpu.VMEM((groups, planes, COLS // 2), bf16),
-            pltpu.VMEM((groups, planes, LANES), bf16),
-            pltpu.VMEM((groups, planes, LANES), bf16),
+            pltpu.VMEM((groups, planes, pixels), bf16),
+            pltpu.VMEM((groups, planes, pixels), bf16),
+            pltpu.VMEM((groups, ROWS, planes, OVL), bf16),
+            pltpu.VMEM((groups, ROWS, planes, OVL), bf16),
+            pltpu.VMEM((planes, pixels), f32),
+            pltpu.VMEM((tiles, planes, COLS // 2), f32),
             pltpu.VMEM((planes, tiles * half_step + LANES), f32),
             dma((4,)), dma((tiles,)), dma((tiles,)),
             dma((groups,)), dma((groups,)), dma((columns,)), dma((columns,)),

time: 20.2 us -> 17.2 us (0.85)
  Pallas kernels: 18 us -> 15 us
    pallas_call x1, Pallas kernels: 18 us -> 15 us  [per_device(): pl.pallas_call(functools.partial(kernel, groups, columns), out_shape=(jax...]
where the time goes in v3:
time: 17.2 us; the launch traced here: 17.1 us
  Pallas kernels  15 us (87%)
  local copies, waits for them, and re-layouts  1.44 us (8%)
  between operations  0.64 us (4%)
    pallas_call x1, Pallas kernels, per_device(): pl.pallas_call(functools.partial(kernel, groups, columns), out_shape=(jax...  15 us
    unnamed x2, local copies, waits for them, and re-layouts  1.44 us

profile of v3, /device:TPU:0, one launch (start us, length us, event | category | flops | bytes accessed | tf_op | source)
XLA Modules:
  0.0 17.1 jit_solution(12171099150445561508)
XLA Ops:
  0.6 15.0 %shard_map.68 = (bf16[4,16,4096]{2,1,0:T(8,128)(2,1)S(1)}, bf16[16,3840]{1,0:T(8,128)(2,1)S(1)}) custom-call(s32[4]{0:T(128)} %counts_hbm.1, s32[128]{0:T(128)} %positions_hbm.1, bf16[4,16,4096]{2,1,0:T(8,128)(2,1)} %raw_hbm.1, bf16[16,4096]{1,0:T(8,128)(2,1)} %dark_hbm.1, bf16[8,4096]{1,0:T(8,128)(2,1)} %basis_hbm.1), custom_call_target="tpu_custom_call" | custom-call | tf_op jit(solution)/shard_map/pallas_call | solution.py:306
  15.6 0.8 %copy.9 = bf16[4,16,4096]{2,1,0:T(8,128)(2,1)} copy(bf16[4,16,4096]{2,1,0:T(8,128)(2,1)S(1)} %get-tuple-element.8) | data formatting | bytes 1048576
  16.4 0.6 %copy.10 = bf16[1,16,1,3840]{3,1,2,0:T(8,128)(2,1)} copy(bf16[1,16,1,3840]{3,1,2,0:T(8,128)(2,1)S(1)} %bitcast.1) | data formatting | bytes 245760

commit v4 on v3

--- a/solution.py
+++ b/solution.py
@@ -294,6 +294,17 @@
     def _():
         for o in range(groups):
             tail_copy(o).wait_send()
+
+
+def deliver(corrected_ref, pooled_ref, corrected_out, pooled_out, sems):
+    tiles = corrected_ref.shape[0]
+    copies = [pltpu.make_async_copy(pooled_ref, pooled_out, sems.at[tiles])]
+    for t in range(tiles):
+        copies.append(pltpu.make_async_copy(corrected_ref.at[t], corrected_out.at[t], sems.at[t]))
+    for copy in copies:
+        copy.start()
+    for copy in copies:
+        copy.wait()
 
 
 def per_device(groups, columns, raw, dark, basis, counts, positions):
@@ -337,6 +348,17 @@
             collective_id=0, has_side_effects=True, vmem_limit_bytes=16 << 20
         ),
     )(*[pltpu.with_memory_space_constraint(x, pltpu.HBM) for x in (counts, positions, raw, dark, basis)])
+    corrected, pooled = pl.pallas_call(
+        deliver,
+        out_shape=(
+            jax.ShapeDtypeStruct(corrected.shape, bf16),
+            jax.ShapeDtypeStruct(pooled.shape, bf16),
+        ),
+        in_specs=[anywhere] * 2,
+        out_specs=(anywhere, anywhere),
+        scratch_shapes=[dma((tiles + 1,))],
+        compiler_params=pltpu.CompilerParams(vmem_limit_bytes=1 << 20),
+    )(corrected, pooled)
     return corrected, pooled.reshape(1, planes, ROWS // 2, tiles * half_step)
 
 

time: 17.2 us -> 16.6 us (0.965)
  local copies, waits for them, and re-layouts: 1.44 us -> 0 us
  Pallas kernels: 15 us -> 15.9 us
    unnamed x2 -> x0, local copies, waits for them, and re-layouts: 1.44 us -> none
    pallas_call x0 -> x1, Pallas kernels: none -> 0.87 us  [per_device(): pl.pallas_call(deliver, out_shape=(jax.ShapeDtypeStruct(corrected.shape,...]
where the time goes in v4:
time: 16.6 us; the launch traced here: 16.5 us
  Pallas kernels  15.9 us (96%)
  between operations  0.64 us (4%)
    pallas_call x1, Pallas kernels, per_device(): pl.pallas_call(functools.partial(kernel, groups, columns), out_shape=(jax...  15 us
    pallas_call x1, Pallas kernels, per_device(): pl.pallas_call(deliver, out_shape=(jax.ShapeDtypeStruct(corrected.shape,...  0.87 us

profile of v4, /device:TPU:0, one launch (start us, length us, event | category | flops | bytes accessed | tf_op | source)
XLA Modules:
  0.0 16.5 jit_solution(7850018728385970753)
XLA Ops:
  0.6 15.0 %shard_map.68 = (bf16[4,16,4096]{2,1,0:T(8,128)(2,1)S(1)}, bf16[16,3840]{1,0:T(8,128)(2,1)S(1)}) custom-call(s32[4]{0:T(128)} %counts_hbm.1, s32[128]{0:T(128)} %positions_hbm.1, bf16[4,16,4096]{2,1,0:T(8,128)(2,1)} %raw_hbm.1, bf16[16,4096]{1,0:T(8,128)(2,1)} %dark_hbm.1, bf16[8,4096]{1,0:T(8,128)(2,1)} %basis_hbm.1), custom_call_target="tpu_custom_call" | custom-call | tf_op jit(solution)/shard_map/pallas_call | solution.py:317
  15.6 0.9 %shard_map.69 = (bf16[4,16,4096]{2,1,0:T(8,128)(2,1)}, bf16[16,3840]{1,0:T(8,128)(2,1)}) custom-call(bf16[4,16,4096]{2,1,0:T(8,128)(2,1)S(1)} %get-tuple-element.6.corrected_ref, bf16[16,3840]{1,0:T(8,128)(2,1)S(1)} %get-tuple-element.7.pooled_ref), custom_call_target="tpu_custom_call" | custom-call | tf_op jit(solution)/shard_map/pallas_call | solution.py:351

commit v5 on v4

--- a/solution.py
+++ b/solution.py
@@ -50,9 +50,7 @@
     g = lax.axis_index("grp")
     d = lax.axis_index("dev")
 
-    raw_loads = [
-        pltpu.make_async_copy(raw_hbm.at[t], raw_ref.at[t], raw_sem.at[t]) for t in range(tiles)
-    ]
+    raw_loads = [pltpu.make_async_copy(raw_hbm, raw_ref, raw_sem.at[0])]
     loads = [
         pltpu.make_async_copy(basis_hbm, rhs.at[0:rank], in_sem.at[0]),
         pltpu.make_async_copy(dark_hbm, dark_ref, in_sem.at[1]),
@@ -97,6 +95,19 @@
     half = planes // 2
     grp_buf[g] = stat[0:half, :] + pltpu.roll(stat[half:, :], LANES // 2, 1)
 
+    pl.semaphore_wait(barrier, 3 * (groups - 1) + columns - 1)
+
+    sent = []
+    for o in range(1, groups):
+        other = lax.rem(g + o, groups)
+        copy = pltpu.make_async_remote_copy(
+            src_ref=grp_buf.at[g], dst_ref=grp_buf.at[g],
+            send_sem=grp_send.at[o], recv_sem=grp_recv.at[g],
+            device_id=(other, d), device_id_type=MESH,
+        )
+        copy.start()
+        sent.append(copy)
+
     def home(at):
         return lax.div(at, band_size), lax.rem(at, tiles)
 
@@ -112,19 +123,6 @@
         for row in range(ROWS):
             tail_out[b, row] = masked[:, (row + 1) * COLS - OVL:(row + 1) * COLS]
     arrived[g] = outgoing[g]
-
-    pl.semaphore_wait(barrier, 3 * (groups - 1) + columns - 1)
-
-    sent = []
-    for o in range(1, groups):
-        other = lax.rem(g + o, groups)
-        copy = pltpu.make_async_remote_copy(
-            src_ref=grp_buf.at[g], dst_ref=grp_buf.at[g],
-            send_sem=grp_send.at[o], recv_sem=grp_recv.at[g],
-            device_id=(other, d), device_id_type=MESH,
-        )
-        copy.start()
-        sent.append(copy)
 
     def cell_copy(o):
         other = lax.rem(g + o, groups)
@@ -199,10 +197,7 @@
             fixed = (raw_ref[t, :, span].astype(jnp.float32) - dark) * inverse
             corrected_ref[t, :, span] = jnp.where(live[t], fixed, 0.0).astype(jnp.bfloat16)
 
-    stores = [
-        pltpu.make_async_copy(corrected_ref.at[t], corrected_hbm.at[t], out_sem.at[t])
-        for t in range(tiles)
-    ]
+    stores = [pltpu.make_async_copy(corrected_ref, corrected_hbm, out_sem.at[0])]
     for copy in stores:
         copy.start()
     for o in range(1, groups):
@@ -340,7 +335,7 @@
             pltpu.VMEM((planes, pixels), f32),
             pltpu.VMEM((tiles, planes, COLS // 2), f32),
             pltpu.VMEM((planes, tiles * half_step + LANES), f32),
-            dma((4,)), dma((tiles,)), dma((tiles,)),
+            dma((4,)), dma((1,)), dma((1,)),
             dma((groups,)), dma((groups,)), dma((columns,)), dma((columns,)),
             dma((groups,)), dma((groups,)), dma((groups,)), dma((groups,)),
         ],

time: 16.6 us -> 16.4 us (0.988)
  Pallas kernels: 15.9 us -> 15.6 us
    pallas_call x1, Pallas kernels: 15 us -> 14.7 us  [per_device(): pl.pallas_call(functools.partial(kernel, groups, columns), out_shape=(jax...]
where the time goes in v5:
time: 16.4 us; the launch traced here: 16.2 us
  Pallas kernels  15.6 us (95%)
  between operations  0.64 us (4%)
    pallas_call x1, Pallas kernels, per_device(): pl.pallas_call(functools.partial(kernel, groups, columns), out_shape=(jax...  14.7 us
    pallas_call x1, Pallas kernels, per_device(): pl.pallas_call(deliver, out_shape=(jax.ShapeDtypeStruct(corrected.shape,...  0.87 us

profile of v5, /device:TPU:0, one launch (start us, length us, event | category | flops | bytes accessed | tf_op | source)
XLA Modules:
  0.0 16.2 jit_solution(15354887946657544459)
XLA Ops:
  0.6 14.7 %shard_map.68 = (bf16[4,16,4096]{2,1,0:T(8,128)(2,1)S(1)}, bf16[16,3840]{1,0:T(8,128)(2,1)S(1)}) custom-call(s32[4]{0:T(128)} %counts_hbm.1, s32[128]{0:T(128)} %positions_hbm.1, bf16[4,16,4096]{2,1,0:T(8,128)(2,1)} %raw_hbm.1, bf16[16,4096]{1,0:T(8,128)(2,1)} %dark_hbm.1, bf16[8,4096]{1,0:T(8,128)(2,1)} %basis_hbm.1), custom_call_target="tpu_custom_call" | custom-call | tf_op jit(solution)/shard_map/pallas_call | solution.py:312
  15.4 0.9 %shard_map.69 = (bf16[4,16,4096]{2,1,0:T(8,128)(2,1)}, bf16[16,3840]{1,0:T(8,128)(2,1)}) custom-call(bf16[4,16,4096]{2,1,0:T(8,128)(2,1)S(1)} %get-tuple-element.6.corrected_ref, bf16[16,3840]{1,0:T(8,128)(2,1)S(1)} %get-tuple-element.7.pooled_ref), custom_call_target="tpu_custom_call" | custom-call | tf_op jit(solution)/shard_map/pallas_call | solution.py:346

commit v6 on v5

--- a/solution.py
+++ b/solution.py
@@ -37,7 +37,7 @@
     counts_hbm, positions_hbm, raw_hbm, dark_hbm, basis_hbm,
     corrected_hbm, pooled_ref,
     counts_ref, positions_ref, raw_ref, dark_ref, rhs, corrected_ref,
-    stat, grp_buf, dev_buf, weights, outgoing, arrived, tail_out, tail_in, inverse_ref, placed, acc,
+    stat, grp_buf, dev_buf, weights, outgoing, arrived, tail_out, tail_in, inverse_ref, placed, acc, diff, stack,
     in_sem, raw_sem, out_sem,
     grp_send, grp_recv, dev_send, dev_recv, cell_send, cell_recv, tail_send, tail_recv,
 ):
@@ -148,6 +148,11 @@
     for o in range(1, groups):
         cell_copy(o).start()
 
+    for i in range(3):
+        stack[i * rank:(i + 1) * rank, :] = rhs[0:rank, :]
+    for t in range(tiles):
+        bare = raw_ref[t].astype(jnp.float32) - dark_ref[...].astype(jnp.float32)
+        diff[t] = jnp.where(wide < counts_ref[t], bare, 0.0)
     for o in range(1, groups):
         source = lax.rem(g + groups - o, groups)
         pltpu.make_async_remote_copy(
@@ -181,21 +186,13 @@
     low = (rest - middle.astype(jnp.float32)).astype(jnp.bfloat16)
 
     parts = jnp.concatenate([low, middle, high], axis=1)
-    plane = lax.broadcasted_iota(jnp.int32, (planes, BLOCK), 0)
-    live = [plane < counts_ref[t] for t in range(tiles)]
     for block in range(pixels // BLOCK):
         span = slice(block * BLOCK, (block + 1) * BLOCK)
-        basis = rhs[0:rank, span]
-        shade = jnp.dot(
-            parts, jnp.concatenate([basis, basis, basis], axis=0),
-            preferred_element_type=jnp.float32,
-        )
+        shade = jnp.dot(parts, stack[:, span], preferred_element_type=jnp.float32)
         inverse = jnp.exp(-shade)
         inverse_ref[:, span] = inverse
-        dark = dark_ref[:, span].astype(jnp.float32)
         for t in range(tiles):
-            fixed = (raw_ref[t, :, span].astype(jnp.float32) - dark) * inverse
-            corrected_ref[t, :, span] = jnp.where(live[t], fixed, 0.0).astype(jnp.bfloat16)
+            corrected_ref[t, :, span] = (diff[t, :, span] * inverse).astype(jnp.bfloat16)
 
     stores = [pltpu.make_async_copy(corrected_ref, corrected_hbm, out_sem.at[0])]
     for copy in stores:
@@ -335,12 +332,14 @@
             pltpu.VMEM((planes, pixels), f32),
             pltpu.VMEM((tiles, planes, COLS // 2), f32),
             pltpu.VMEM((planes, tiles * half_step + LANES), f32),
+            pltpu.VMEM(raw.shape, f32),
+            pltpu.VMEM((3 * basis.shape[0], pixels), bf16),
             dma((4,)), dma((1,)), dma((1,)),
             dma((groups,)), dma((groups,)), dma((columns,)), dma((columns,)),
             dma((groups,)), dma((groups,)), dma((groups,)), dma((groups,)),
         ],
         compiler_params=pltpu.CompilerParams(
-            collective_id=0, has_side_effects=True, vmem_limit_bytes=16 << 20
+            collective_id=0, has_side_effects=True, vmem_limit_bytes=24 << 20
         ),
     )(*[pltpu.with_memory_space_constraint(x, pltpu.HBM) for x in (counts, positions, raw, dark, basis)])
     corrected, pooled = pl.pallas_call(

time: 16.4 us -> 16.4 us (level)
  no operation moved by 1% of the time
where the time goes in v6:
time: 16.4 us; the launch traced here: 16.2 us
  Pallas kernels  15.6 us (95%)
  between operations  0.64 us (4%)
    pallas_call x1, Pallas kernels, per_device(): pl.pallas_call(functools.partial(kernel, groups, columns), out_shape=(jax...  14.7 us
    pallas_call x1, Pallas kernels, per_device(): pl.pallas_call(deliver, out_shape=(jax.ShapeDtypeStruct(corrected.shape,...  0.87 us

profile of v6, /device:TPU:0, one launch (start us, length us, event | category | flops | bytes accessed | tf_op | source)
XLA Modules:
  0.0 16.2 jit_solution(191223037586505417)
XLA Ops:
  0.6 14.7 %shard_map.68 = (bf16[4,16,4096]{2,1,0:T(8,128)(2,1)S(1)}, bf16[16,3840]{1,0:T(8,128)(2,1)S(1)}) custom-call(s32[4]{0:T(128)} %counts_hbm.1, s32[128]{0:T(128)} %positions_hbm.1, bf16[4,16,4096]{2,1,0:T(8,128)(2,1)} %raw_hbm.1, bf16[16,4096]{1,0:T(8,128)(2,1)} %dark_hbm.1, bf16[8,4096]{1,0:T(8,128)(2,1)} %basis_hbm.1), custom_call_target="tpu_custom_call" | custom-call | tf_op jit(solution)/shard_map/pallas_call | solution.py:309
  15.4 0.9 %shard_map.69 = (bf16[4,16,4096]{2,1,0:T(8,128)(2,1)}, bf16[16,3840]{1,0:T(8,128)(2,1)}) custom-call(bf16[4,16,4096]{2,1,0:T(8,128)(2,1)S(1)} %get-tuple-element.6.corrected_ref, bf16[16,3840]{1,0:T(8,128)(2,1)S(1)} %get-tuple-element.7.pooled_ref), custom_call_target="tpu_custom_call" | custom-call | tf_op jit(solution)/shard_map/pallas_call | solution.py:345

commit v7 on v6

--- a/solution.py
+++ b/solution.py
@@ -113,7 +113,7 @@
 
     wide = lax.broadcasted_iota(jnp.int32, (planes, pixels), 0)
     mine = [home(positions_ref[(g * columns + d) * tiles + t]) for t in range(tiles)]
-    for b in range(groups):
+    def build(b):
         chosen = pick((mine[t][0] == b, t) for t in range(tiles))
         masked = jnp.where(
             wide < counts_ref[chosen],
@@ -122,7 +122,6 @@
         outgoing[b] = masked
         for row in range(ROWS):
             tail_out[b, row] = masked[:, (row + 1) * COLS - OVL:(row + 1) * COLS]
-    arrived[g] = outgoing[g]
 
     def cell_copy(o):
         other = lax.rem(g + o, groups)
@@ -140,13 +139,16 @@
             device_id=(other, lax.rem(d + 1, columns)), device_id_type=MESH,
         )
 
+    for o in range(1, groups):
+        build(lax.rem(g + o, groups))
+        cell_copy(o).start()
+    build(g)
+    arrived[g] = outgoing[g]
+
     @pl.when(d < columns - 1)
     def _():
         for o in range(groups):
             tail_copy(o).start()
-
-    for o in range(1, groups):
-        cell_copy(o).start()
 
     for i in range(3):
         stack[i * rank:(i + 1) * rank, :] = rhs[0:rank, :]

time: 16.4 us -> 16.2 us (0.988)
  Pallas kernels: 15.6 us -> 15.3 us
    pallas_call x1, Pallas kernels: 14.7 us -> 14.4 us  [per_device(): pl.pallas_call(functools.partial(kernel, groups, columns), out_shape=(jax...]
where the time goes in v7:
time: 16.2 us; the launch traced here: 16 us
  Pallas kernels  15.3 us (94%)
  between operations  0.64 us (4%)
    pallas_call x1, Pallas kernels, per_device(): pl.pallas_call(functools.partial(kernel, groups, columns), out_shape=(jax...  14.4 us
    pallas_call x1, Pallas kernels, per_device(): pl.pallas_call(deliver, out_shape=(jax.ShapeDtypeStruct(corrected.shape,...  0.87 us

profile of v7, /device:TPU:0, one launch (start us, length us, event | category | flops | bytes accessed | tf_op | source)
XLA Modules:
  0.0 16.0 jit_solution(4182514596191052741)
XLA Ops:
  0.6 14.4 %shard_map.68 = (bf16[4,16,4096]{2,1,0:T(8,128)(2,1)S(1)}, bf16[16,3840]{1,0:T(8,128)(2,1)S(1)}) custom-call(s32[4]{0:T(128)} %counts_hbm.1, s32[128]{0:T(128)} %positions_hbm.1, bf16[4,16,4096]{2,1,0:T(8,128)(2,1)} %raw_hbm.1, bf16[16,4096]{1,0:T(8,128)(2,1)} %dark_hbm.1, bf16[8,4096]{1,0:T(8,128)(2,1)} %basis_hbm.1), custom_call_target="tpu_custom_call" | custom-call | tf_op jit(solution)/shard_map/pallas_call | solution.py:311
  15.1 0.9 %shard_map.69 = (bf16[4,16,4096]{2,1,0:T(8,128)(2,1)}, bf16[16,3840]{1,0:T(8,128)(2,1)}) custom-call(bf16[4,16,4096]{2,1,0:T(8,128)(2,1)S(1)} %get-tuple-element.6.corrected_ref, bf16[16,3840]{1,0:T(8,128)(2,1)S(1)} %get-tuple-element.7.pooled_ref), custom_call_target="tpu_custom_call" | custom-call | tf_op jit(solution)/shard_map/pallas_call | solution.py:347
